TPU v7x, 32 devices: a whole 2x2x4 slice. The times are simulated.
32 devices in a mesh: parts: 2 (over x), chol: 16 (over z, y, core).
Axes of the slice: x: 2, y: 2, z: 4, core: 2. Of those that a mesh axis runs over, the one named last changes fastest.
Arguments:
- orbitals: float32 [32, 100, 1024], P(('parts', 'chol')), parts along dimension 0, may hold values from -6 to 6
- intersection_inv: float32 [32, 100, 100], P(('parts', 'chol')), parts along dimension 0, may hold values from -0.625 to 0.625
- factor_rows: bfloat16 [4096, 1024], P('chol'), may hold values from -0.1875 to 0.1875
- factor_rotated: bfloat16 [100, 4096], replicated, may hold values from -0.625 to 0.625
- factor_core: bfloat16 [1024, 4096], P('chol'), may hold values from -0.125 to 0.125
- fields: float32 [32, 1024], P('parts', 'chol'), parts along dimension 0, may hold values from -6 to 6
Outputs:
- propagated: float32 [32, 100, 1024], P(('parts', 'chol')), parts along dimension 0
- force_bias: float32 [32, 1024], P('parts', 'chol'), parts along dimension 0
There are 2 independent parts, one for each index of `parts`. A program takes and returns all parts, laid end to end along the dimension named above; an argument that names none is the same for every part. Nothing has to cross between parts.
All inputs are finite; a program needn't handle non-finite values.
Results may differ from a plain program's by a relative error of at most 0.0091.
Values may be sent and summed in bfloat16 or wider, within the bound.
A program may use at most 64 MiB of HBM per device.

v0:
```python
import jax
import jax.numpy as jnp
from jax import lax
from jax.sharding import PartitionSpec as P

TAYLOR = 4


def density_one(half_green, all_rows, factor_rotated):
    projected = lax.dot_general(
        half_green, all_rows, (((1,), (1,)), ((), ())), preferred_element_type=jnp.float32
    )
    return jnp.sum(factor_rotated.astype(jnp.float32) * projected, axis=0).astype(jnp.bfloat16)


def propagate_one(orbital, potential, all_rows):
    total = orbital
    term = orbital
    for order in range(1, TAYLOR + 1):
        summed = lax.dot_general(
            term.astype(jnp.bfloat16),
            all_rows,
            (((1,), (1,)), ((), ())),
            preferred_element_type=jnp.float32,
        )
        scaled = (summed * potential[None, :] / order).astype(jnp.bfloat16)
        term = jnp.dot(scaled, all_rows, preferred_element_type=jnp.float32)
        total = total + term
    return total


def on_device(orbitals, intersection_inv, factor_rows, factor_rotated, factor_core, fields):
    walker_count = orbitals.shape[0]
    half_green = jnp.einsum(
        "wij,wjm->wim", intersection_inv, orbitals, precision=lax.Precision.HIGHEST
    ).astype(jnp.bfloat16)
    all_rows = lax.all_gather(factor_rows, "chol", axis=0, tiled=True)
    own_density = lax.map(lambda item: density_one(item, all_rows, factor_rotated), half_green)
    density = lax.all_gather(own_density, "chol", axis=0, tiled=True)
    force_bias = lax.dot_general(
        density, factor_core, (((1,), (1,)), ((), ())), preferred_element_type=jnp.float32
    )
    shifted = (fields - force_bias).astype(jnp.bfloat16)
    partial_sum = jnp.dot(shifted, factor_core, preferred_element_type=jnp.float32)
    summed_all = lax.psum(partial_sum, "chol")
    potential = lax.dynamic_slice_in_dim(
        summed_all, lax.axis_index("chol") * walker_count, walker_count, 0
    )
    propagated = lax.map(
        lambda pair: propagate_one(pair[0], pair[1], all_rows), (orbitals, potential)
    )
    return (propagated, force_bias)


def solution(mesh):
    in_specs = (
        P(("parts", "chol"), None, None),
        P(("parts", "chol"), None, None),
        P("chol", None),
        P(),
        P("chol", None),
        P("parts", "chol"),
    )
    out_specs = (P(("parts", "chol"), None, None), P("parts", "chol"))
    return jax.shard_map(
        on_device, mesh=mesh, in_specs=in_specs, out_specs=out_specs, check_vma=False
    )
```

profile of v0, /device:TPU:0, one launch (start us, length us, event | category | flops | bytes accessed | tf_op | source)
XLA Modules:
  0.0 249.2 jit_solution(8666170632495442712)
XLA Ops:
  7.2 0.0 copy-start
  7.2 0.0 copy-start.1
  7.2 0.0 copy-start.3
  7.2 0.0 all-gather.3.cloned.1.call-start
  7.2 0.7 all-gather.3.cloned.1.call-update
  7.9 0.0 all-reduce.2.cloned.1.call-start
  8.0 1.6 convolution_convert_fusion
  9.6 77.7 %all-gather.3.cloned.1.call-done = bf16[4096,1024]{1,0:T(8,128)(2,1)} async-done(((bf16[256,1024]{1,0:T(8,128)(2,1)}), bf16[4096,1024]{1,0:T(8,128)(2,1)}) %all-gather.3.cloned.1.call-update) | async-done | bytes 8388624 | tf_op jit(solution)/shard_map/all_gather | solution.py:37
  87.2 6.3 %fusion.7 = bf16[4096]{0:T(1024)(128)(2,1)S(1)} fusion(bf16[100,1024]{1,0:T(8,128)(2,1)S(1)} %convolution_convert_fusion, bf16[4096,1024]{1,0:T(8,128)(2,1)} %all-gather.3.cloned.1.call-done, bf16[100,4096]{1,0:T(8,128)(2,1)} %param.9), kind=kOutput, calls=%fused_computation.12 | convolution fusion | flops 840085504 | bytes 9420800 | tf_op jit(solution)/shard_map/while/body/eval_jaxpr/dot_general | solution.py:10
  93.5 19.5 %all-gather = bf16[65536]{0:T(1024)(128)(2,1)S(1)} all-gather(bf16[4096]{0:T(1024)(128)(2,1)S(1)} %fusion.7), channel_id=2, replica_groups=mesh['parts'=2,'chol'=16] {'chol'}, dimensions={0}, use_global_device_ids=true | all-gather | bytes 139264 | tf_op jit(solution)/shard_map/all_gather | solution.py:39
  113.0 0.1 reshape.20
  113.1 0.0 copy-done
  113.1 0.2 fusion.28
  113.3 0.0 copy-done.3
  113.3 0.0 copy-start.2
  113.3 0.9 fusion.24
  114.2 0.0 all-reduce.2.cloned.1.call-update
  114.3 87.1 %all-reduce.2.cloned.1.call-done = f32[16,4096]{1,0:T(8,128)} async-done(((f32[16,4096]{1,0:T(8,128)}), f32[16,4096]{1,0:T(8,128)}) %all-reduce.2.cloned.1.call-update) | async-done | bytes 262160 | tf_op jit(solution)/shard_map/psum | solution.py:45
  201.4 0.9 constant_dynamic-slice_fusion
  202.3 0.0 copy-done.1
  202.3 9.7 %fusion.11 = f32[100,1024]{1,0:T(8,128)S(1)} fusion(bf16[4096,1024]{1,0:T(8,128)(2,1)} %all-gather.3.cloned.1.call-done, f32[4096]{0:T(1024)S(1)} %bitcast.32, f32[1,100,1024]{2,0,1:T(1,128)S(1)} %copy-done.1), kind=kOutput, calls=%fused_computation.18 | convolution fusion | flops 1678540800 | bytes 9224192 | tf_op jit(solution)/shard_map/while/body/eval_jaxpr/dot_general | solution.py:27
  212.0 0.0 copy-done.2
  212.0 9.7 %fusion.10 = f32[100,1024]{1,0:T(8,128)S(1)} fusion(bf16[4096,1024]{1,0:T(8,128)(2,1)} %all-gather.3.cloned.1.call-done, f32[4096]{0:T(1024)S(1)} %bitcast.33, f32[100,1024]{1,0:T(8,128)S(1)} %fusion.11), kind=kOutput, calls=%fused_computation.17 | convolution fusion | flops 1679052800 | bytes 9224192 | tf_op jit(solution)/shard_map/while/body/eval_jaxpr/dot_general | solution.py:27
  221.7 9.7 %fusion.9 = f32[100,1024]{1,0:T(8,128)S(1)} fusion(bf16[4096,1024]{1,0:T(8,128)(2,1)} %all-gather.3.cloned.1.call-done, f32[4096]{0:T(1024)S(1)} %bitcast.34, f32[100,1024]{1,0:T(8,128)S(1)} %fusion.10), kind=kOutput, calls=%fused_computation.16 | convolution fusion | flops 1679052800 | bytes 9224192 | tf_op jit(solution)/shard_map/while/body/eval_jaxpr/dot_general | solution.py:27
  231.5 9.7 %fusion.8 = f32[1,100,1024]{2,1,0:T(8,128)S(1)} fusion(bf16[4096,1024]{1,0:T(8,128)(2,1)} %all-gather.3.cloned.1.call-done, f32[4096]{0:T(1024)S(1)} %bitcast.35, f32[100,1024]{1,0:T(8,128)S(1)} %fusion.9, f32[100,1024]{1,0:T(8,128)S(1)} %fusion.10, f32[100,1024]{1,0:T(8,128)S(1)} %fusion.11, f32[1,100,1024]{2,0,1:T(1,128)S(1)} %copy-done.1), kind=kOutput, calls=%fused_computation.14 | convolution fusion | flops 1679462400 | bytes 10452992 | tf_op jit(solution)/shard_map/while/body/eval_jaxpr/dot_general | solution.py:27
  241.2 1.2 copy.9
Async XLA Ops:
  7.2 105.9 %copy-start = (bf16[64,4096]{1,0:T(8,128)(2,1)S(1)}, bf16[64,4096]{1,0:T(8,128)(2,1)}, u32[]{:S(2)}) copy-start(bf16[64,4096]{1,0:T(8,128)(2,1)} %param.10) | copy-start | bytes 1572868
  7.2 195.2 %copy-start.1 = (f32[1,100,1024]{2,0,1:T(1,128)S(1)}, f32[1,100,1024]{2,0,1:T(1,128)}, u32[]{:S(2)}) copy-start(f32[1,100,1024]{2,0,1:T(1,128)} %param.6) | copy-start | bytes 1228804
  7.2 106.1 %copy-start.3 = (f32[16,64]{1,0:T(8,128)S(1)}, f32[16,64]{1,0:T(8,128)}, u32[]{:S(2)}) copy-start(f32[16,64]{1,0:T(8,128)} %param.11) | copy-start | bytes 12292
  7.2 80.0 %all-gather.3.cloned.1.call-start = ((), (), s32[]{:S(2)}) async-start(), calls=%async_computation | async-start | bytes 8912896 | tf_op jit(solution)/shard_map/all_gather | solution.py:37
  7.9 193.5 %all-reduce.2.cloned.1.call-start = ((), (), s32[]{:S(2)}) async-start(), calls=%async_computation.1 | async-start | bytes 524288 | tf_op jit(solution)/shard_map/psum | solution.py:45
  113.3 98.7 %copy-start.2 = (f32[16,64]{1,0:T(8,128)}, f32[16,64]{1,0:T(8,128)S(1)}, u32[]{:S(2)}) copy-start(f32[16,64]{1,0:T(8,128)S(1)} %fusion.28) | copy-start | bytes 12292
Sparse Core Ops, SparseCore 0:
  10.2 77.0 all-gather.2
  114.4 86.9 all-reduce.1
where the time goes:
time: 249 us
  waiting for transfers between devices  166 us (67%)
  matrix products  47.9 us (19%)
  blocking collectives  19.5 us (8%)
  between operations  14.1 us (6%)
    psum x1, waiting for transfers between devices, on_device(): summed_all = lax.psum(partial_sum, 'chol')  87.1 us
    all_gather x1, waiting for transfers between devices, on_device(): all_rows = lax.all_gather(factor_rows, 'chol', axis=0, tiled=True)  77.7 us
    dot_general x4, matrix products, propagate_one(): term = jnp.dot(scaled, all_rows, preferred_element_type=jnp.float32)  38.9 us
    all_gather x1, blocking collectives, on_device(): density = lax.all_gather(own_density, 'chol', axis=0, tiled=True)  19.5 us
    dot_general x1, matrix products, density_one(): lax.dot_general(half_green, all_rows, (((1,), (1,)), ((), ())), preferred...  6.26 us
  transfers between devices with their start and end apart: 2, of which 2 were waited for; matrix products, arithmetic and copies ran while one was open for 1% of the time, Pallas kernels for 0%

commit v1 on v0

--- a/solution.py
+++ b/solution.py
@@ -42,7 +42,11 @@
     )
     shifted = (fields - force_bias).astype(jnp.bfloat16)
     partial_sum = jnp.dot(shifted, factor_core, preferred_element_type=jnp.float32)
-    summed_all = lax.psum(partial_sum, "chol")
+    summed_all = partial_sum
+    for hop in (1, 2, 4, 8):
+        summed_all = summed_all + lax.ppermute(
+            summed_all, "chol", [(dev, dev ^ hop) for dev in range(16)]
+        )
     potential = lax.dynamic_slice_in_dim(
         summed_all, lax.axis_index("chol") * walker_count, walker_count, 0
     )

time: 249 us -> 192 us (0.77)
  waiting for transfers between devices: 166 us -> 109 us
    psum x1 -> x0, waiting for transfers between devices: 87.1 us -> none  [on_device(): summed_all = lax.psum(partial_sum, 'chol')]
    ppermute x0 -> x4, waiting for transfers between devices: none -> 30.6 us  [on_device(): lax.ppermute(summed_all, 'chol', [(dev, dev ^ hop) for dev in range(16)])]
  transfers between devices with their start and end apart: 2 -> 5, of which waited for: 2 -> 5; matrix products, arithmetic and copies ran while one was open for 1% -> 1% of each run, Pallas kernels for 0% -> 0%
where the time goes in v1:
time: 192 us
  waiting for transfers between devices  109 us (57%)
  matrix products  47.1 us (25%)
  blocking collectives  19.5 us (10%)
  between operations  14.1 us (7%)
    all_gather x1, waiting for transfers between devices, on_device(): all_rows = lax.all_gather(factor_rows, 'chol', axis=0, tiled=True)  77.7 us
    dot_general x4, matrix products, propagate_one(): term = jnp.dot(scaled, all_rows, preferred_element_type=jnp.float32)  38.8 us
    ppermute x4, waiting for transfers between devices, on_device(): lax.ppermute(summed_all, 'chol', [(dev, dev ^ hop) for dev in range(16)])  30.6 us
    all_gather x1, blocking collectives, on_device(): density = lax.all_gather(own_density, 'chol', axis=0, tiled=True)  19.5 us
    dot_general x1, matrix products, density_one(): lax.dot_general(half_green, all_rows, (((1,), (1,)), ((), ())), preferred...  6.26 us
  transfers between devices with their start and end apart: 5, of which 5 were waited for; matrix products, arithmetic and copies ran while one was open for 1% of the time, Pallas kernels for 0%

profile of v1, /device:TPU:0, one launch (start us, length us, event | category | flops | bytes accessed | tf_op | source)
XLA Modules:
  0.0 191.9 jit_solution(5680352916425631144)
XLA Ops:
  7.2 0.0 copy-start
  7.2 0.0 copy-start.1
  7.2 0.0 copy-start.3
  7.2 0.0 all-gather.3.cloned.1.call-start
  7.2 0.7 all-gather.3.cloned.1.call-update
  7.9 1.6 convolution_convert_fusion
  9.5 77.7 %all-gather.3.cloned.1.call-done = bf16[4096,1024]{1,0:T(8,128)(2,1)} async-done(((bf16[256,1024]{1,0:T(8,128)(2,1)}), bf16[4096,1024]{1,0:T(8,128)(2,1)}) %all-gather.3.cloned.1.call-update) | async-done | bytes 8388624 | tf_op jit(solution)/shard_map/all_gather | solution.py:37
  87.2 6.3 %fusion.7 = bf16[4096]{0:T(1024)(128)(2,1)S(1)} fusion(bf16[100,1024]{1,0:T(8,128)(2,1)S(1)} %convolution_convert_fusion, bf16[4096,1024]{1,0:T(8,128)(2,1)} %all-gather.3.cloned.1.call-done, bf16[100,4096]{1,0:T(8,128)(2,1)} %param.9), kind=kOutput, calls=%fused_computation.12 | convolution fusion | flops 840085504 | bytes 9420800 | tf_op jit(solution)/shard_map/while/body/eval_jaxpr/dot_general | solution.py:10
  93.5 19.5 %all-gather = bf16[65536]{0:T(1024)(128)(2,1)S(1)} all-gather(bf16[4096]{0:T(1024)(128)(2,1)S(1)} %fusion.7), channel_id=2, replica_groups=mesh['parts'=2,'chol'=16] {'chol'}, dimensions={0}, use_global_device_ids=true | all-gather | bytes 139264 | tf_op jit(solution)/shard_map/all_gather | solution.py:39
  113.0 0.1 reshape.20
  113.1 0.0 copy-done
  113.1 0.2 fusion.28
  113.3 0.0 copy-done.3
  113.3 0.0 copy-start.2
  113.3 0.2 fusion.24
  113.5 0.4 collective-permute-start
  113.9 1.2 collective-permute-done
  115.2 0.2 collective-permute-start.1
  115.4 8.4 %collective-permute-done.1 = f32[16,4096]{1,0:T(8,128)S(1)} collective-permute-done((f32[16,4096]{1,0:T(8,128)S(1)}, f32[16,4096]{1,0:T(8,128)S(1)}, u32[]{:S(2)}, u32[]{:S(2)}) %collective-permute-start.1) | collective-permute-done | bytes 262176 | tf_op jit(solution)/shard_map/ppermute | solution.py:47
  123.8 0.1 collective-permute-start.2
  123.9 7.7 %collective-permute-done.2 = f32[16,4096]{1,0:T(8,128)S(1)} collective-permute-done((f32[16,4096]{1,0:T(8,128)S(1)}, f32[16,4096]{1,0:T(8,128)S(1)}, u32[]{:S(2)}, u32[]{:S(2)}) %collective-permute-start.2) | collective-permute-done | bytes 262176 | tf_op jit(solution)/shard_map/ppermute | solution.py:47
  131.6 0.1 collective-permute-start.3
  131.7 13.3 %collective-permute-done.3 = f32[16,4096]{1,0:T(8,128)S(1)} collective-permute-done((f32[16,4096]{1,0:T(8,128)S(1)}, f32[16,4096]{1,0:T(8,128)S(1)}, u32[]{:S(2)}, u32[]{:S(2)}) %collective-permute-start.3) | collective-permute-done | bytes 262176 | tf_op jit(solution)/shard_map/ppermute | solution.py:47
  145.1 0.0 copy-done.1
  145.1 9.7 %fusion.11 = f32[100,1024]{1,0:T(8,128)S(1)} fusion(bf16[4096,1024]{1,0:T(8,128)(2,1)} %all-gather.3.cloned.1.call-done, f32[4096]{0:T(1024)S(1)} %bitcast.32, f32[1,100,1024]{2,0,1:T(1,128)S(1)} %copy-done.1), kind=kOutput, calls=%fused_computation.18 | convolution fusion | flops 1678540800 | bytes 9224192 | tf_op jit(solution)/shard_map/while/body/eval_jaxpr/dot_general | solution.py:27
  154.7 0.0 copy-done.2
  154.8 9.7 %fusion.10 = f32[100,1024]{1,0:T(8,128)S(1)} fusion(bf16[4096,1024]{1,0:T(8,128)(2,1)} %all-gather.3.cloned.1.call-done, f32[4096]{0:T(1024)S(1)} %bitcast.33, f32[100,1024]{1,0:T(8,128)S(1)} %fusion.11), kind=kOutput, calls=%fused_computation.17 | convolution fusion | flops 1679052800 | bytes 9224192 | tf_op jit(solution)/shard_map/while/body/eval_jaxpr/dot_general | solution.py:27
  164.4 9.7 %fusion.9 = f32[100,1024]{1,0:T(8,128)S(1)} fusion(bf16[4096,1024]{1,0:T(8,128)(2,1)} %all-gather.3.cloned.1.call-done, f32[4096]{0:T(1024)S(1)} %bitcast.34, f32[100,1024]{1,0:T(8,128)S(1)} %fusion.10), kind=kOutput, calls=%fused_computation.16 | convolution fusion | flops 1679052800 | bytes 9224192 | tf_op jit(solution)/shard_map/while/body/eval_jaxpr/dot_general | solution.py:27
  174.2 9.7 %fusion.8 = f32[1,100,1024]{2,1,0:T(8,128)S(1)} fusion(bf16[4096,1024]{1,0:T(8,128)(2,1)} %all-gather.3.cloned.1.call-done, f32[4096]{0:T(1024)S(1)} %bitcast.35, f32[100,1024]{1,0:T(8,128)S(1)} %fusion.9, f32[100,1024]{1,0:T(8,128)S(1)} %fusion.10, f32[100,1024]{1,0:T(8,128)S(1)} %fusion.11, f32[1,100,1024]{2,0,1:T(1,128)S(1)} %copy-done.1), kind=kOutput, calls=%fused_computation.14 | convolution fusion | flops 1679462400 | bytes 10452992 | tf_op jit(solution)/shard_map/while/body/eval_jaxpr/dot_general | solution.py:27
  183.9 1.2 copy.9
  (4 shorter events, 0.1 us)
Async XLA Ops:
  7.2 105.9 %copy-start = (bf16[64,4096]{1,0:T(8,128)(2,1)S(1)}, bf16[64,4096]{1,0:T(8,128)(2,1)}, u32[]{:S(2)}) copy-start(bf16[64,4096]{1,0:T(8,128)(2,1)} %param.10) | copy-start | bytes 1572868
  7.2 137.9 %copy-start.1 = (f32[1,100,1024]{2,0,1:T(1,128)S(1)}, f32[1,100,1024]{2,0,1:T(1,128)}, u32[]{:S(2)}) copy-start(f32[1,100,1024]{2,0,1:T(1,128)} %param.6) | copy-start | bytes 1228804
  7.2 106.1 %copy-start.3 = (f32[16,64]{1,0:T(8,128)S(1)}, f32[16,64]{1,0:T(8,128)}, u32[]{:S(2)}) copy-start(f32[16,64]{1,0:T(8,128)} %param.11) | copy-start | bytes 12292
  7.2 80.0 %all-gather.3.cloned.1.call-start = ((), (), s32[]{:S(2)}) async-start(), calls=%async_computation | async-start | bytes 8912896 | tf_op jit(solution)/shard_map/all_gather | solution.py:37
  113.3 41.4 %copy-start.2 = (f32[16,64]{1,0:T(8,128)}, f32[16,64]{1,0:T(8,128)S(1)}, u32[]{:S(2)}) copy-start(f32[16,64]{1,0:T(8,128)S(1)} %fusion.28) | copy-start | bytes 12292
  113.5 1.6 collective-permute-start
  115.2 8.6 %collective-permute-start.1 = (f32[16,4096]{1,0:T(8,128)S(1)}, f32[16,4096]{1,0:T(8,128)S(1)}, u32[]{:S(2)}, u32[]{:S(2)}) collective-permute-start(f32[16,4096]{1,0:T(8,128)S(1)} %add.35), channel_id=1, source_target_pairs={{0,2},{1,3},{2,0},{3,1},{4,6},{5,7},{6,4},{7,5},{8,10},{9,11},{10,... | collective-permute-start | bytes 786440 | tf_op jit(solution)/shard_map/ppermute | solution.py:47
  123.8 7.8 %collective-permute-start.2 = (f32[16,4096]{1,0:T(8,128)S(1)}, f32[16,4096]{1,0:T(8,128)S(1)}, u32[]{:S(2)}, u32[]{:S(2)}) collective-permute-start(f32[16,4096]{1,0:T(8,128)S(1)} %add.36), channel_id=1, source_target_pairs={{0,4},{1,5},{2,6},{3,7},{4,0},{5,1},{6,2},{7,3},{8,12},{9,13},{10,... | collective-permute-start | bytes 786440 | tf_op jit(solution)/shard_map/ppermute | solution.py:47
  131.6 13.4 %collective-permute-start.3 = (f32[16,4096]{1,0:T(8,128)S(1)}, f32[16,4096]{1,0:T(8,128)S(1)}, u32[]{:S(2)}, u32[]{:S(2)}) collective-permute-start(f32[16,4096]{1,0:T(8,128)S(1)} %add.37), channel_id=1, source_target_pairs={{0,8},{1,9},{2,10},{3,11},{4,12},{5,13},{6,14},{7,15},{8,0},{9,1},... | collective-permute-start | bytes 786440 | tf_op jit(solution)/shard_map/ppermute | solution.py:47
Sparse Core Ops, SparseCore 0:
  10.2 77.0 all-gather.2
